TPU v7x, 512 devices: a whole 4x8x8 slice. The times are simulated.
512 devices in a mesh: dp: 32 (over x, y), table: 16 (over z, core).
Axes of the slice: x: 4, y: 8, z: 8, core: 2. Of those that a mesh axis runs over, the one named last changes fastest.
Arguments:
- table: bfloat16 [12288, 512], P('table'), may hold values from -6 to 6
- history_shard: int32 [512, 256, 1], P(('dp', 'table')), may hold values from 0 to 15; in each aligned block of 256 rows (0 to 255, 256 to 511, ..., all dimensions but the last counted through in order) at most 32 rows name the same one
- history_row: int32 [512, 256], P(('dp', 'table')), may hold values from 0 to 767
- lengths: int32 [512], P(('dp', 'table')), may hold values from 1 to 256, 98304 in all
- w_in: bfloat16 [512, 2048], replicated, may hold values from -0.25 to 0.25
- w_out: bfloat16 [512, 512], replicated, may hold values from -0.25 to 0.25
- cotangent: bfloat16 [512, 256, 512], P(('dp', 'table')), may hold values from -6 to 6
Outputs:
- table_grad: float32 [12288, 512], P('table')
- dense_grad: bfloat16 [512, 512], replicated
Inputs may be any that keep to these rules, and one draw needn't show every extreme that they name: `history_shard`: among the 256 history slots of one device's samples, at most 32 name one table shard, and that bound is met by some shard in some device's slots. `lengths`: some sample has the full length 256.
All inputs are finite; a program needn't handle non-finite values. No bound on the sum of `lengths` on one device may be relied on, other than what follows from the above.
Results may differ from a plain program's by a relative error of at most 0.017.
Values may be sent and summed in bfloat16 or wider, within the bound.
A program may use at most 64 MiB of HBM per device.

v0:
```python
import math
import jax
import jax.numpy as jnp
from jax import lax
from jax.sharding import PartitionSpec as P

HEADS = 4


def layer_norm(values):
    average = jnp.mean(values, axis=-1, keepdims=True)
    centred = values - average
    variance = jnp.mean(centred * centred, axis=-1, keepdims=True)
    return centred * lax.rsqrt(variance + 1e-06)


def hstu_layer(embedded, w_in, w_out, lengths):
    samples_here, seq_span, model_width = embedded.shape
    head_dim = model_width // HEADS
    normed = layer_norm(embedded.astype(jnp.float32)).astype(jnp.bfloat16)
    projected = jax.nn.silu(
        jnp.dot(
            normed.reshape(samples_here * seq_span, model_width),
            w_in,
            preferred_element_type=jnp.float32,
        )
    )
    gate_part = projected[:, :model_width]
    shaped = (samples_here, seq_span, HEADS, head_dim)
    values = projected[:, model_width : 2 * model_width].astype(jnp.bfloat16).reshape(shaped)
    queries = projected[:, 2 * model_width : 3 * model_width].astype(jnp.bfloat16).reshape(shaped)
    keys = projected[:, 3 * model_width :].astype(jnp.bfloat16).reshape(shaped)
    scores = jnp.einsum(
        "blhd,bmhd->bhlm", queries.astype(jnp.float32), keys.astype(jnp.float32)
    ) * head_dim ** (-0.5)
    positions = jnp.arange(seq_span)
    live_keys = (positions[None, None, :] <= positions[None, :, None]) & (
        positions[None, None, :] < lengths[:, None, None]
    )
    weights = (
        jnp.where(live_keys[:, None], jax.nn.silu(scores), 0.0)
        / lengths.astype(jnp.float32)[:, None, None, None]
    )
    weights = weights.astype(jnp.bfloat16)
    attended = jnp.einsum(
        "bhlm,bmhd->blhd", weights.astype(jnp.float32), values.astype(jnp.float32)
    ).reshape(samples_here * seq_span, model_width)
    mixed = (layer_norm(attended) * gate_part).astype(jnp.bfloat16)
    output = jnp.dot(mixed, w_out, preferred_element_type=jnp.float32) + embedded.reshape(
        -1, model_width
    ).astype(jnp.float32)
    return (output, mixed)


def per_device(table, history_shard, history_row, lengths, w_in, w_out, cotangent):
    shard_rows, model_width = table.shape
    samples_here, seq_span = history_row.shape
    groups = lax.axis_size("table")
    slot_count = samples_here * seq_span
    capacity = 2 * slot_count // groups
    owners = history_shard[:, :, 0].reshape(-1)
    local_rows = history_row.reshape(-1)
    owner_hits = (owners[:, None] == jnp.arange(groups)[None, :]).astype(jnp.int32)
    slot_rank = jnp.sum((jnp.cumsum(owner_hits, axis=0) - owner_hits) * owner_hits, axis=1)
    position = owners * capacity + slot_rank
    requested = (
        jnp.zeros((groups * capacity,), jnp.int32)
        .at[position]
        .set(local_rows)
        .reshape(groups, capacity)
    )
    incoming = lax.all_to_all(requested, "table", split_axis=0, concat_axis=0, tiled=True).reshape(
        -1
    )
    global_rows = owners * shard_rows + local_rows
    piece = lax.all_gather(table, "table", axis=0, tiled=True)
    inside = (global_rows >= 0) & (global_rows < piece.shape[0])
    taken = piece[jnp.clip(global_rows, 0, piece.shape[0] - 1)].astype(jnp.float32)
    embedded = jnp.where(inside[:, None], taken, 0.0).astype(jnp.bfloat16)
    embedded = embedded.reshape(samples_here, seq_span, model_width)
    output, pullback, mixed = jax.vjp(
        lambda rows_in: hstu_layer(rows_in, w_in, w_out, lengths), embedded, has_aux=True
    )
    row_live = jnp.arange(seq_span)[None, :] < lengths[:, None]
    grad_seed = jnp.where(row_live[:, :, None], cotangent, jnp.zeros_like(cotangent))
    flat_seed = grad_seed.reshape(-1, model_width)
    (row_grad,) = pullback(flat_seed.astype(jnp.float32))
    dense_part = jnp.dot(mixed.T, flat_seed, preferred_element_type=jnp.float32)
    outgoing = (
        jnp.zeros((groups * capacity, model_width), jnp.bfloat16)
        .at[position]
        .set(row_grad.reshape(-1, model_width))
    )
    arrived = lax.all_to_all(
        outgoing.reshape(groups, capacity, model_width),
        "table",
        split_axis=0,
        concat_axis=0,
        tiled=True,
    )
    local_grad = (
        jnp.zeros((shard_rows, model_width), jnp.float32)
        .at[incoming]
        .add(arrived.reshape(-1, model_width).astype(jnp.float32))
    )
    total_slots = slot_count * lax.axis_size("dp") * groups
    grad_scale = 1.0 / math.sqrt(total_slots)
    table_grad = lax.psum(local_grad, "dp")
    dense_total = lax.psum(dense_part, ("dp", "table"))
    dense_grad = (dense_total * grad_scale).astype(jnp.bfloat16)
    return (table_grad, dense_grad)


def solution(mesh):
    in_specs = (
        P("table", None),
        P(("dp", "table"), None, None),
        P(("dp", "table"), None),
        P(("dp", "table")),
        P(),
        P(),
        P(("dp", "table"), None, None),
    )
    out_specs = (P("table", None), P())
    return jax.shard_map(
        per_device, mesh=mesh, in_specs=in_specs, out_specs=out_specs, check_vma=False
    )
```

profile of v0, /device:TPU:64, one launch (start us, length us, event | category | flops | bytes accessed | tf_op | source)
XLA Modules:
  0.0 582.9 jit_solution(10138484838293075610)
XLA Ops:
  7.2 0.7 all-gather.2.cloned.1.call-update
  7.9 0.7 fusion.64
  8.6 0.6 reduce-window.6
  9.2 0.2 slice_reduce_fusion
  9.4 0.8 fusion.63
  10.2 0.7 compare_select_fusion.1
  10.9 1.6 scatter_custom_fusion
  12.4 0.7 all_to_all.9
  13.1 10.0 %all-to-all-start = ((s32[16,1,32]{2,1,0:T(1,128)}), s32[16,1,32]{2,1,0:T(1,128)S(1)}, u32[]{:S(2)}, u32[]{:S(2)}) async-start(s32[16,1,32]{2,1,0:T(1,128)} %all_to_all.9), calls=%async_computation | async-start | bytes 16384 | tf_op jit(solution)/shard_map/all_to_all | solution.py:72
  23.8 0.7 compare_and_fusion
  24.5 66.3 %all-gather.2.cloned.1.call-done = bf16[12288,512]{1,0:T(8,128)(2,1)} async-done(((bf16[768,512]{1,0:T(8,128)(2,1)}), bf16[12288,512]{1,0:T(8,128)(2,1)}) %all-gather.2.cloned.1.call-update) | async-done | bytes 12582928 | tf_op jit(solution)/shard_map/all_gather | solution.py:76
  90.8 7.4 %gather_fusion = bf16[256,512]{1,0:T(8,128)(2,1)S(1)} fusion(bf16[12288,512]{1,0:T(8,128)(2,1)} %all-gather.2.cloned.1.call-done, s32[1024]{0:T(1024)S(1)} %pad_clamp_fusion), kind=kCustom, calls=%fused_computation | custom fusion | bytes 525312 | tf_op jit(solution)/shard_map/gather | solution.py:78
  98.2 0.2 convert_reduce_fusion
  98.4 0.2 fusion.38
  98.7 2.8 fusion.76
  101.5 0.8 slice_bitcast_fusion
  102.2 0.1 copy.40
  102.4 0.1 copy.41
  102.5 1.6 divide_convert_fusion
  104.1 0.3 fusion.78
  104.5 0.1 fusion.40
  104.6 0.3 copy-done.2
  104.9 0.2 copy.35
  105.1 1.7 multiply_reduce_fusion.1
  106.9 2.1 fusion.75
  108.9 0.1 broadcast_add_fusion
  109.0 0.1 copy.36
  109.2 2.0 fusion.26
  111.3 0.2 fusion.80
  111.5 1.0 fusion.79
  112.5 0.9 fusion.81
  113.5 0.1 copy.37
  113.6 1.8 copy.38
  115.4 1.8 copy.39
  117.2 3.4 multiply_reduce_fusion
  120.6 1.0 fusion.74
  121.6 2.9 scatter_custom_fusion.1
  124.5 6.9 %all-to-all-start.1 = ((bf16[16,32,512]{2,1,0:T(8,128)(2,1)}), bf16[16,32,512]{2,1,0:T(8,128)(2,1)}, u32[]{:S(2)}, u32[]{:S(2)}) async-start(bf16[16,32,512]{2,1,0:T(8,128)(2,1)} %bitcast.120), calls=%async_computation.1 | async-start | bytes 1048576 | tf_op jit(solution)/shard_map/all_to_all | solution.py:94
  131.4 0.2 all-reduce.9.cloned.1.call-start
  131.6 2.5 fusion.45
  134.2 0.5 broadcast.379
  134.7 0.7 reduce.15
  135.4 10.4 %all-to-all-done.1 = bf16[16,32,512]{2,1,0:T(8,128)(2,1)} async-done(((bf16[16,32,512]{2,1,0:T(8,128)(2,1)}), bf16[16,32,512]{2,1,0:T(8,128)(2,1)}, u32[]{:S(2)}, u32[]{:S(2)}) %all-to-all-start.1) | async-done | bytes 524320 | tf_op jit(solution)/shard_map/all_to_all | solution.py:94
  145.8 5.5 scatter_custom_fusion.2
  151.3 258.6 %all-reduce.9.cloned.1.call-done = f32[512,512]{1,0:T(8,128)} async-done(((f32[512,512]{1,0:T(8,128)}), f32[512,512]{1,0:T(8,128)}) %all-reduce.9.cloned.1.call-update) | async-done | bytes 1048592 | tf_op jit(solution)/shard_map/psum | solution.py:109
  409.9 2.1 multiply_convert_fusion
  412.0 161.6 %all-reduce.7.cloned.1.call-done = f32[768,512]{1,0:T(8,128)} async-done(((f32[768,512]{1,0:T(8,128)}), f32[768,512]{1,0:T(8,128)}) %all-reduce.7.cloned.1.call-update) | async-done | bytes 1572880 | tf_op jit(solution)/shard_map/psum | solution.py:108
  573.7 2.7 copy.58
  (36 shorter events, 0.4 us)
Async XLA Ops:
  7.2 91.5 %copy-start = (bf16[512,2048]{1,0:T(8,128)(2,1)S(1)}, bf16[512,2048]{1,0:T(8,128)(2,1)}, u32[]{:S(2)}) copy-start(bf16[512,2048]{1,0:T(8,128)(2,1)} %param.11) | copy-start | bytes 6291460
  7.2 83.6 %all-gather.2.cloned.1.call-start = ((), (), s32[]{:S(2)}) async-start(), calls=%async_computation.2 | async-start | bytes 13369344 | tf_op jit(solution)/shard_map/all_gather | solution.py:76
  13.1 111.4 %all-to-all-start = ((s32[16,1,32]{2,1,0:T(1,128)}), s32[16,1,32]{2,1,0:T(1,128)S(1)}, u32[]{:S(2)}, u32[]{:S(2)}) async-start(s32[16,1,32]{2,1,0:T(1,128)} %all_to_all.9), calls=%async_computation | async-start | bytes 16384 | tf_op jit(solution)/shard_map/all_to_all | solution.py:72
  102.4 1.8 copy-start.4
  102.5 1.6 copy-start.6
  102.5 1.6 copy-start.8
  104.1 0.8 copy-start.2
  109.2 2.1 copy-start.5
  109.2 2.3 copy-start.7
  111.2 1.3 copy-start.3
  117.2 4.4 copy-start.1
  124.5 21.3 %all-to-all-start.1 = ((bf16[16,32,512]{2,1,0:T(8,128)(2,1)}), bf16[16,32,512]{2,1,0:T(8,128)(2,1)}, u32[]{:S(2)}, u32[]{:S(2)}) async-start(bf16[16,32,512]{2,1,0:T(8,128)(2,1)} %bitcast.120), calls=%async_computation.1 | async-start | bytes 1048576 | tf_op jit(solution)/shard_map/all_to_all | solution.py:94
  131.4 278.5 %all-reduce.9.cloned.1.call-start = ((), (), s32[]{:S(2)}) async-start(), calls=%async_computation.4 | async-start | bytes 2097152 | tf_op jit(solution)/shard_map/psum | solution.py:109
  134.1 439.6 %all-reduce.7.cloned.1.call-start = ((), (), s32[]{:S(2)}) async-start(), calls=%async_computation.3 | async-start | bytes 3145728 | tf_op jit(solution)/shard_map/psum | solution.py:108
Sparse Core Ops, SparseCore 0:
  10.1 80.5 all-gather.1
  137.3 272.5 all-reduce.8
  414.3 159.3 all-reduce.6
where the time goes:
time: 584 us; the launch traced here: 583 us
  waiting for transfers between devices  498 us (85%)
  local copies, waits for them, and re-layouts  18.5 us (3%)
  other arithmetic  18.5 us (3%)
  starting transfers between devices  17.1 us (3%)
  matrix products  16.5 us (3%)
  between operations  14.6 us (2%)
    psum x1, waiting for transfers between devices, per_device(): dense_total = lax.psum(dense_part, ('dp', 'table'))  259 us
    psum x1, waiting for transfers between devices, per_device(): table_grad = lax.psum(local_grad, 'dp')  162 us
    all_gather x1, waiting for transfers between devices, per_device(): piece = lax.all_gather(table, 'table', axis=0, tiled=True)  66.3 us
  transfers between devices with their start and end apart: 5, of which 4 were waited for; matrix products, arithmetic and copies ran while one was open for 9% of the time, Pallas kernels for 0%

commit v1 on v0

--- a/solution.py
+++ b/solution.py
@@ -105,7 +105,11 @@
     )
     total_slots = slot_count * lax.axis_size("dp") * groups
     grad_scale = 1.0 / math.sqrt(total_slots)
-    table_grad = lax.psum(local_grad, "dp")
+    table_grad = local_grad
+    for hop in (1, 2, 4, 8, 16):
+        table_grad = table_grad + lax.ppermute(
+            table_grad, "dp", [(dev, dev ^ hop) for dev in range(32)]
+        )
     dense_total = lax.psum(dense_part, ("dp", "table"))
     dense_grad = (dense_total * grad_scale).astype(jnp.bfloat16)
     return (table_grad, dense_grad)

time: 584 us -> 672 us (1.15)
  the two profiles are of different devices: /device:TPU:64 before, /device:TPU:24 now
where the time goes in v1:
time: 672 us; the launch traced here: 671 us
  waiting for transfers between devices  565 us (84%)
  starting transfers between devices  32.7 us (5%)
  other arithmetic  25.7 us (4%)
  matrix products  16.5 us (2%)
  local copies, waits for them, and re-layouts  15.8 us (2%)
  between operations  15 us (2%)
    psum x1, waiting for transfers between devices, per_device(): dense_total = lax.psum(dense_part, ('dp', 'table'))  269 us
    ppermute x5, waiting for transfers between devices, per_device(): lax.ppermute(table_grad, 'dp', [(dev, dev ^ hop) for dev in range(32)])  212 us
    all_gather x1, waiting for transfers between devices, per_device(): piece = lax.all_gather(table, 'table', axis=0, tiled=True)  68.7 us
    ppermute x5, starting transfers between devices, per_device(): lax.ppermute(table_grad, 'dp', [(dev, dev ^ hop) for dev in range(32)])  17.8 us
    all_to_all x1, waiting for transfers between devices, per_device(): lax.all_to_all(outgoing.reshape(groups, capacity, model_width), 'table',...  14.6 us
  transfers between devices with their start and end apart: 9, of which 7 were waited for; matrix products, arithmetic and copies ran while one was open for 7% of the time, Pallas kernels for 0%

profile of v1, /device:TPU:24, one launch (start us, length us, event | category | flops | bytes accessed | tf_op | source)
XLA Modules:
  0.0 670.9 jit_solution(5140011026267119332)
XLA Ops:
  7.2 0.7 all-gather.2.cloned.1.call-update
  7.9 0.7 fusion.64
  8.6 0.6 reduce-window.6
  9.4 0.8 fusion.63
  10.2 0.7 compare_select_fusion.1
  10.9 1.6 scatter_custom_fusion
  12.4 0.7 all_to_all.9
  13.1 10.4 %all-to-all-start = ((s32[16,1,32]{2,1,0:T(1,128)}), s32[16,1,32]{2,1,0:T(1,128)S(1)}, u32[]{:S(2)}, u32[]{:S(2)}) async-start(s32[16,1,32]{2,1,0:T(1,128)} %all_to_all.9), calls=%async_computation | async-start | bytes 16384 | tf_op jit(solution)/shard_map/all_to_all | solution.py:72
  24.2 0.7 compare_and_fusion
  25.0 68.7 %all-gather.2.cloned.1.call-done = bf16[12288,512]{1,0:T(8,128)(2,1)} async-done(((bf16[768,512]{1,0:T(8,128)(2,1)}), bf16[12288,512]{1,0:T(8,128)(2,1)}) %all-gather.2.cloned.1.call-update) | async-done | bytes 12582928 | tf_op jit(solution)/shard_map/all_gather | solution.py:76
  93.6 7.4 %gather_fusion = bf16[256,512]{1,0:T(8,128)(2,1)S(1)} fusion(bf16[12288,512]{1,0:T(8,128)(2,1)} %all-gather.2.cloned.1.call-done, s32[1024]{0:T(1024)S(1)} %pad_clamp_fusion), kind=kCustom, calls=%fused_computation | custom fusion | bytes 525312 | tf_op jit(solution)/shard_map/gather | solution.py:78
  101.5 2.8 fusion.76
  104.3 0.8 slice_bitcast_fusion
  105.4 1.6 divide_convert_fusion
  107.0 0.3 fusion.78
  107.5 0.3 copy-done.2
  108.0 1.7 multiply_reduce_fusion.1
  109.7 2.1 fusion.75
  112.1 2.0 fusion.26
  114.4 1.0 fusion.79
  115.4 0.9 fusion.81
  116.5 1.8 copy.38
  118.3 1.8 copy.39
  120.1 3.4 multiply_reduce_fusion
  123.4 1.0 fusion.74
  124.5 2.9 scatter_custom_fusion.1
  127.4 4.2 all-to-all-start.1
  131.9 0.5 broadcast.379
  132.4 0.7 reduce.15
  133.1 14.6 %all-to-all-done.1 = bf16[16,32,512]{2,1,0:T(8,128)(2,1)} async-done(((bf16[16,32,512]{2,1,0:T(8,128)(2,1)}), bf16[16,32,512]{2,1,0:T(8,128)(2,1)}, u32[]{:S(2)}, u32[]{:S(2)}) %all-to-all-start.1) | async-done | bytes 524320 | tf_op jit(solution)/shard_map/all_to_all | solution.py:94
  147.7 5.3 scatter_custom_fusion.2
  153.0 2.4 collective-permute-start
  155.5 36.2 %collective-permute-done = f32[768,512]{1,0:T(8,128)S(1)} collective-permute-done((f32[768,512]{1,0:T(8,128)}, f32[768,512]{1,0:T(8,128)S(1)}, u32[]{:S(2)}, u32[]{:S(2)}) %collective-permute-start) | collective-permute-done | bytes 1572896 | tf_op jit(solution)/shard_map/ppermute | solution.py:110
  191.7 1.8 add.132
  193.4 2.4 collective-permute-start.1
  195.8 70.9 %collective-permute-done.1 = f32[768,512]{1,0:T(8,128)S(1)} collective-permute-done((f32[768,512]{1,0:T(8,128)S(1)}, f32[768,512]{1,0:T(8,128)S(1)}, u32[]{:S(2)}, u32[]{:S(2)}) %collective-permute-start.1) | collective-permute-done | bytes 1572896 | tf_op jit(solution)/shard_map/ppermute | solution.py:110
  266.8 0.3 add.133
  267.1 4.7 collective-permute-start.2
  271.8 70.3 %collective-permute-done.2 = f32[768,512]{1,0:T(8,128)S(1)} collective-permute-done((f32[768,512]{1,0:T(8,128)S(1)}, f32[768,512]{1,0:T(8,128)S(1)}, u32[]{:S(2)}, u32[]{:S(2)}) %collective-permute-start.2) | collective-permute-done | bytes 1572896 | tf_op jit(solution)/shard_map/ppermute | solution.py:110
  342.1 0.3 add.134
  342.5 3.4 collective-permute-start.3
  345.8 34.9 %collective-permute-done.3 = f32[768,512]{1,0:T(8,128)S(1)} collective-permute-done((f32[768,512]{1,0:T(8,128)S(1)}, f32[768,512]{1,0:T(8,128)S(1)}, u32[]{:S(2)}, u32[]{:S(2)}) %collective-permute-start.3) | collective-permute-done | bytes 1572896 | tf_op jit(solution)/shard_map/ppermute | solution.py:110
  380.7 1.5 add.135
  382.2 4.9 collective-permute-start.4
  387.1 2.5 fusion.45
  389.6 269.0 %all-reduce.6.cloned.1.call-done = f32[512,512]{1,0:T(8,128)} async-done(((f32[512,512]{1,0:T(8,128)}), f32[512,512]{1,0:T(8,128)}) %all-reduce.6.cloned.1.call-update) | async-done | bytes 1048592 | tf_op jit(solution)/shard_map/psum | solution.py:113
  658.6 2.1 multiply_convert_fusion
  660.7 3.4 add.136
  (47 shorter events, 2.3 us)
Async XLA Ops:
  7.2 94.4 %copy-start = (bf16[512,2048]{1,0:T(8,128)(2,1)S(1)}, bf16[512,2048]{1,0:T(8,128)(2,1)}, u32[]{:S(2)}) copy-start(bf16[512,2048]{1,0:T(8,128)(2,1)} %param.11) | copy-start | bytes 6291460
  7.2 86.5 %all-gather.2.cloned.1.call-start = ((), (), s32[]{:S(2)}) async-start(), calls=%async_computation.2 | async-start | bytes 13369344 | tf_op jit(solution)/shard_map/all_gather | solution.py:76
  13.1 114.3 %all-to-all-start = ((s32[16,1,32]{2,1,0:T(1,128)}), s32[16,1,32]{2,1,0:T(1,128)S(1)}, u32[]{:S(2)}, u32[]{:S(2)}) async-start(s32[16,1,32]{2,1,0:T(1,128)} %all_to_all.9), calls=%async_computation | async-start | bytes 16384 | tf_op jit(solution)/shard_map/all_to_all | solution.py:72
  105.2 1.8 copy-start.4
  105.4 1.6 copy-start.6
  105.4 1.6 copy-start.8
  107.0 0.8 copy-start.2
  112.0 2.1 copy-start.5
  112.1 2.3 copy-start.7
  114.1 1.3 copy-start.3
  120.1 4.4 copy-start.1
  127.4 20.3 %all-to-all-start.1 = ((bf16[16,32,512]{2,1,0:T(8,128)(2,1)}), bf16[16,32,512]{2,1,0:T(8,128)(2,1)}, u32[]{:S(2)}, u32[]{:S(2)}) async-start(bf16[16,32,512]{2,1,0:T(8,128)(2,1)} %bitcast.120), calls=%async_computation.1 | async-start | bytes 1048576 | tf_op jit(solution)/shard_map/all_to_all | solution.py:94
  131.6 526.9 %all-reduce.6.cloned.1.call-start = ((), (), s32[]{:S(2)}) async-start(), calls=%async_computation.3 | async-start | bytes 2097152 | tf_op jit(solution)/shard_map/psum | solution.py:113
  153.0 38.6 %collective-permute-start = (f32[768,512]{1,0:T(8,128)}, f32[768,512]{1,0:T(8,128)S(1)}, u32[]{:S(2)}, u32[]{:S(2)}) collective-permute-start(f32[768,512]{1,0:T(8,128)} %scatter_custom_fusion.2), channel_id=1, source_target_pairs={{0,16},{16,0},{32,48},{48,32},{64,80},{80,64},{96,112},{112,96},{1... | collective-permute-start | bytes 4718600 | tf_op jit(solution)/shard_map/ppermute | solution.py:110
  193.4 73.3 %collective-permute-start.1 = (f32[768,512]{1,0:T(8,128)S(1)}, f32[768,512]{1,0:T(8,128)S(1)}, u32[]{:S(2)}, u32[]{:S(2)}) collective-permute-start(f32[768,512]{1,0:T(8,128)S(1)} %add.132), channel_id=1, source_target_pairs={{0,32},{16,48},{32,0},{48,16},{64,96},{80,112},{96,64},{112,80},{1... | collective-permute-start | bytes 4718600 | tf_op jit(solution)/shard_map/ppermute | solution.py:110
  267.1 75.0 %collective-permute-start.2 = (f32[768,512]{1,0:T(8,128)S(1)}, f32[768,512]{1,0:T(8,128)S(1)}, u32[]{:S(2)}, u32[]{:S(2)}) collective-permute-start(f32[768,512]{1,0:T(8,128)S(1)} %add.133), channel_id=1, source_target_pairs={{0,64},{16,80},{32,96},{48,112},{64,0},{80,16},{96,32},{112,48},{1... | collective-permute-start | bytes 4718600 | tf_op jit(solution)/shard_map/ppermute | solution.py:110
  342.5 38.2 %collective-permute-start.3 = (f32[768,512]{1,0:T(8,128)S(1)}, f32[768,512]{1,0:T(8,128)S(1)}, u32[]{:S(2)}, u32[]{:S(2)}) collective-permute-start(f32[768,512]{1,0:T(8,128)S(1)} %add.134), channel_id=1, source_target_pairs={{0,128},{16,144},{32,160},{48,176},{64,192},{80,208},{96,224},{112... | collective-permute-start | bytes 4718600 | tf_op jit(solution)/shard_map/ppermute | solution.py:110
  382.2 278.5 %collective-permute-start.4 = (f32[768,512]{1,0:T(8,128)}, f32[768,512]{1,0:T(8,128)}, u32[]{:S(2)}, u32[]{:S(2)}) collective-permute-start(f32[768,512]{1,0:T(8,128)} %add.135), channel_id=1, source_target_pairs={{0,256},{16,272},{32,288},{48,304},{64,320},{80,336},{96,352},{112... | collective-permute-start | bytes 4718600 | tf_op jit(solution)/shard_map/ppermute | solution.py:110
Sparse Core Ops, SparseCore 0:
  10.1 83.4 all-gather.1
  389.7 268.8 all-reduce.5
